TPU v7x, 256 devices: a whole 4x4x8 slice. The times are simulated.
256 devices in a mesh: prow: 16 (over x, y), pcol: 16 (over z, core).
Axes of the slice: x: 4, y: 4, z: 8, core: 2. Of those that a mesh axis runs over, the one named last changes fastest.
Arguments:
- ainv: float32 [16384, 16384], P('prow', 'pcol'), as said below
- panels: float32 [3, 16384, 512], P(None, 'prow', 'pcol'), may hold values from -0.53 to 0.53
- pattern: int32 [3, 128], replicated, may hold values 0 or 1
- coupling: float32 [3, 512, 512], replicated, may hold values from -0.25 to 0.25
- dinv: float32 [3, 512, 512], replicated, as said below
Outputs:
- xpanel: float32 [3, 16384, 512], P(None, 'prow', 'pcol')
- xcross: float32 [3, 512, 512], P(None, 'pcol')
- ydiag: float32 [3, 512, 512], P(None, 'pcol')
Inputs may be any that keep to these rules, and one draw needn't show every extreme that they name: ainv is symmetric: ainv equals its transpose up to rounding. Each dinv[k] is symmetric: it equals its transpose exactly.
All inputs are finite; a program needn't handle non-finite values.
Results may differ from a plain program's by a relative error of at most 0.000092.
Values sent between devices are 32-bit elements; how exact they have to be, the bound alone decides.
A program may use at most 128 MiB of HBM per device.

v0:
```python
import jax
import jax.numpy as jnp
from jax import lax
from jax.sharding import PartitionSpec as P

NB = 128
high = lax.Precision.HIGH
highest = lax.Precision.HIGHEST


def mm(left, right, precision=high):
    return jnp.dot(left, right, precision=precision, preferred_element_type=jnp.float32)


def tmm(left, right, precision=high):
    return lax.dot_general(
        left,
        right,
        (((0,), (0,)), ((), ())),
        precision=precision,
        preferred_element_type=jnp.float32,
    )


def mmt(left, right, precision=high):
    return lax.dot_general(
        left,
        right,
        (((1,), (1,)), ((), ())),
        precision=precision,
        preferred_element_type=jnp.float32,
    )


def shards(ainv, panels, pattern, coupling, dinv):
    rows = lax.axis_size("prow")
    cols = lax.axis_size("pcol")
    row_index = lax.axis_index("prow")
    col_index = lax.axis_index("pcol")
    count, depth, width = panels.shape
    blocks_here = depth // NB
    flags = lax.dynamic_slice_in_dim(pattern, row_index * blocks_here, blocks_here, 1)
    row_mask = jnp.repeat(flags.astype(jnp.float32), NB, axis=1)
    factors = jnp.swapaxes(panels, 1, 2) * row_mask[:, None, :]
    f0, f1, f2 = lax.all_gather(factors, "pcol", axis=1, tiled=True)
    c0, c1, c2 = (coupling[0], coupling[1], coupling[2])
    u01 = -c0
    u12 = -c2
    u02 = mm(c0, c2, highest) - c1
    h0 = f0
    h1 = f1 + tmm(u01, f0)
    h2 = f2 + tmm(u02, f0) + tmm(u12, f1)
    ht = jnp.concatenate([h0, h1, h2], 0)
    partial = mm(ht, ainv).reshape(count, rows, width, depth)
    mine = lax.psum_scatter(partial, "prow", scatter_dimension=1, tiled=False)
    perm = [(r * cols + c, c * cols + r) for r in range(rows) for c in range(cols)]
    xt = -lax.ppermute(mine, ("prow", "pcol"), perm)
    inner0 = mmt(xt[0], ht)
    inner1 = mmt(xt[1], ht[512:])
    inner2 = mmt(xt[2], ht[1024:])
    summed = lax.psum(jnp.concatenate([inner0, inner1, inner2], 1), "prow")
    start = col_index * width

    def own(matrix, axis):
        return lax.dynamic_slice_in_dim(matrix, start, width, axis)

    d0 = own(dinv[0], 0)
    a01 = tmm(own(u01, 1), dinv[0], highest)
    a02 = tmm(own(u02, 1), dinv[0], highest)
    b1 = own(dinv[1], 0)
    b12 = tmm(own(u12, 1), dinv[1], highest)
    y0 = d0 - summed[:, 0:512]
    e01 = mm(d0, u01, highest) - summed[:, 512:1024]
    e02 = mm(d0, u02, highest) - summed[:, 1024:1536]
    y1 = b1 + mm(a01, u01, highest) - summed[:, 1536:2048]
    e12 = mm(a01, u02, highest) + mm(b1, u12, highest) - summed[:, 2048:2560]
    y2 = own(dinv[2], 0) + mm(a02, u02, highest) + mm(b12, u12, highest) - summed[:, 2560:3072]
    return (jnp.swapaxes(xt, 1, 2), jnp.stack([e01, e02, e12], 0), jnp.stack([y0, y1, y2], 0))


def solution(mesh):
    placed = (P("prow", "pcol"), P(None, "prow", "pcol"), P(), P(), P())
    return jax.shard_map(
        shards,
        mesh=mesh,
        in_specs=placed,
        out_specs=(P(None, "prow", "pcol"), P(None, "pcol", None), P(None, "pcol", None)),
        check_vma=False,
    )
```

profile of v0, /device:TPU:2, one launch (start us, length us, event | category | flops | bytes accessed | tf_op | source)
XLA Modules:
  0.0 337.9 jit_solution(12168469248919959419)
XLA Ops:
  7.2 0.0 slice-start
  7.2 0.0 all-gather.2.cloned.1.call-start
  7.2 0.8 dynamic-slice_convert_fusion
  8.1 0.1 broadcast_bitcast_fusion
  8.1 1.8 multiply_bitcast_fusion
  9.9 0.0 all-gather.2.cloned.1.call-update
  10.0 0.0 reduce-scatter.4.cloned.1.call-start
  10.0 0.0 slice-done
  10.0 1.3 copy.12
  11.3 4.8 %convolution_subtract_fusion = f32[512,512]{0,1:T(8,128)} fusion(f32[1,512,512]{1,2,0:T(8,128)} %copy.12, f32[3,512,512]{2,1,0:T(8,128)} %param.8), kind=kOutput, calls=%fused_computation.14 | convolution fusion | flops 1610874880 | bytes 4194304 | tf_op jit(solution)/shard_map/dot_general | solution.py:12
  16.1 43.3 %all-gather.2.cloned.1.call-done = f32[3,512,1024]{2,1,0:T(8,128)} async-done(((f32[3,32,1024]{2,1,0:T(8,128)}), f32[3,512,1024]{2,1,0:T(8,128)}) %all-gather.2.cloned.1.call-update) | async-done | bytes 6291472 | tf_op jit(solution)/shard_map/all_gather | solution.py:45
  59.4 0.0 copy-done
  59.4 4.3 %bitcast_add_fusion = f32[512,1024]{1,0:T(8,128)S(1)} fusion(f32[3,512,1024]{2,1,0:T(8,128)} %all-gather.2.cloned.1.call-done, f32[3,512,512]{2,1,0:T(8,128)S(1)} %copy-done), kind=kOutput, calls=%fused_computation.12 | convolution fusion | flops 1611399168 | bytes 7340032 | tf_op jit(solution)/shard_map/dot_general | solution.py:16
  63.7 0.0 copy-start.6
  63.7 4.0 %slice_bitcast_fusion.2 = f32[512,1024]{1,0:T(8,128)} fusion(f32[3,512,1024]{2,1,0:T(8,128)} %all-gather.2.cloned.1.call-done), kind=kLoop, calls=%fused_computation.11 | loop fusion | bytes 4194304 | tf_op jit(solution)/shard_map/unstack | solution.py:45
  67.7 1.9 fusion.62
  69.7 2.0 fusion.7
  71.8 16.0 %fusion.1 = f32[1536,1024]{1,0:T(8,128)S(1)} fusion(f32[1024,1024]{1,0:T(8,128)} %param.5, f32[512,1024]{1,0:T(8,128)S(1)} %fusion.7, f32[512,1024]{1,0:T(8,128)S(1)} %bitcast_add_fusion, f32[512,1024]{1,0:T(8,128)} %slice_bitcast_fusion.2), kind=kOutput, calls=%fused_computation.2 | convolution fusion | flops 9666822144 | bytes 16777216 | tf_op jit(solution)/shard_map/dot_general | solution.py:12
  87.8 0.0 copy-done.3
  87.8 3.2 copy.11
  91.0 0.0 reduce-scatter.4.cloned.1.call-update
  91.1 0.0 all-reduce.3.cloned.1.call-start
  91.1 0.0 copy-start.2
  91.1 1.3 bitcast_negate_fusion
  92.4 2.0 fusion.21
  94.4 1.0 fusion.65
  95.4 81.0 %reduce-scatter.4.cloned.1.call-done = f32[3,1,32,1024]{3,2,0,1:T(8,128)} async-done(((f32[3,16,32,1024]{3,2,0,1:T(8,128)}), f32[3,1,32,1024]{3,2,0,1:T(8,128)}) %reduce-scatter.4.cloned.1.call-update) | async-done | bytes 393232
  176.5 5.0 %collective-permute-start = (f32[3,32,1024]{2,1,0:T(8,128)}, f32[3,32,1024]{2,1,0:T(8,128)S(1)}, u32[]{:S(2)}, u32[]{:S(2)}) collective-permute-start(f32[3,32,1024]{2,1,0:T(8,128)} %bitcast.108), channel_id=1, source_target_pairs={{0,0},{1,16},{2,32},{3,48},{4,64},{5,80},{6,96},{7,112},{8,128},{9... | collective-permute-start | bytes 1179656 | tf_op jit(solution)/shard_map/ppermute | solution.py:57
  181.4 2.0 fusion.19
  183.4 3.7 %fusion.63 = (f32[1,512,512]{2,1,0:T(8,128)}, f32[1,512,512]{2,1,0:T(8,128)}, f32[1,512,512]{2,1,0:T(8,128)}) fusion(f32[3,512,512]{2,1,0:T(8,128)} %param.9), kind=kLoop, calls=%fused_computation.89 | loop fusion | bytes 6291456 | tf_op jit(solution)/shard_map/slice | solution.py:77
  187.2 29.7 %collective-permute-done = f32[3,32,1024]{2,1,0:T(8,128)S(1)} collective-permute-done((f32[3,32,1024]{2,1,0:T(8,128)}, f32[3,32,1024]{2,1,0:T(8,128)S(1)}, u32[]{:S(2)}, u32[]{:S(2)}) %collective-permute-start) | collective-permute-done | bytes 393248 | tf_op jit(solution)/shard_map/ppermute | solution.py:57
  216.8 0.8 fusion.64
  217.6 0.0 copy-done.8
  217.6 3.0 fusion
  220.6 2.0 fusion.2
  222.6 1.1 fusion.41
  223.7 0.8 pad_maximum_fusion.3
  224.5 0.0 all-reduce.3.cloned.1.call-update
  224.5 2.1 fusion.17
  226.6 2.3 convolution_add_fusion.1
  228.8 92.2 %all-reduce.3.cloned.1.call-done = f32[32,3072]{1,0:T(8,128)} async-done(((f32[32,3072]{1,0:T(8,128)}), f32[32,3072]{1,0:T(8,128)}) %all-reduce.3.cloned.1.call-update) | async-done | bytes 393232 | tf_op jit(solution)/shard_map/psum | solution.py:61
  321.0 2.3 fusion.15
  323.3 1.6 fusion.16
  324.9 0.9 fusion.42
  325.8 1.6 fusion.12
  327.4 1.6 fusion.14
  329.0 1.6 fusion.10
  330.6 0.8 pad_maximum_fusion.4
  (14 shorter events, 0.0 us)
Async XLA Ops:
  7.2 2.8 slice-start
  7.2 52.3 %all-gather.2.cloned.1.call-start = ((), (), s32[]{:S(2)}) async-start(), calls=%async_computation.1 | async-start | bytes 6684672 | tf_op jit(solution)/shard_map/all_gather | solution.py:45
  10.0 166.5 %reduce-scatter.4.cloned.1.call-start = ((), (), s32[]{:S(2)}) async-start(), calls=%async_computation.3 | async-start | bytes 6684672
  11.3 48.1 %copy-start = (f32[3,512,512]{2,1,0:T(8,128)S(1)}, f32[3,512,512]{2,1,0:T(8,128)}, u32[]{:S(2)}) copy-start(f32[3,512,512]{2,1,0:T(8,128)} %param.8) | copy-start | bytes 9437188
  59.4 8.3 %copy-start.5 = (f32[3,512,1024]{2,1,0:T(8,128)S(1)}, f32[3,512,1024]{2,1,0:T(8,128)}, u32[]{:S(2)}) copy-start(f32[3,512,1024]{2,1,0:T(8,128)} %all-gather.2.cloned.1.call-done) | copy-start | bytes 18874372
  63.7 8.0 %copy-start.6 = (f32[512,1024]{1,0:T(8,128)}, f32[512,1024]{1,0:T(8,128)S(1)}, u32[]{:S(2)}) copy-start(f32[512,1024]{1,0:T(8,128)S(1)} %bitcast_add_fusion) | copy-start | bytes 6291460
  63.7 4.0 %copy-start.1 = (f32[512,512]{0,1:T(8,128)S(1)}, f32[512,512]{0,1:T(8,128)}, u32[]{:S(2)}) copy-start(f32[512,512]{0,1:T(8,128)} %convolution_subtract_fusion) | copy-start | bytes 3145732
  71.7 16.0 %copy-start.3 = (f32[512,1024]{1,0:T(8,128)}, f32[512,1024]{1,0:T(8,128)S(1)}, u32[]{:S(2)}) copy-start(f32[512,1024]{1,0:T(8,128)S(1)} %fusion.7) | copy-start | bytes 6291460
  91.1 229.9 %all-reduce.3.cloned.1.call-start = ((), (), s32[]{:S(2)}) async-start(), calls=%async_computation.2 | async-start | bytes 786432 | tf_op jit(solution)/shard_map/psum | solution.py:61
  91.1 3.2 copy-start.2
  176.5 40.4 %collective-permute-start = (f32[3,32,1024]{2,1,0:T(8,128)}, f32[3,32,1024]{2,1,0:T(8,128)S(1)}, u32[]{:S(2)}, u32[]{:S(2)}) collective-permute-start(f32[3,32,1024]{2,1,0:T(8,128)} %bitcast.108), channel_id=1, source_target_pairs={{0,0},{1,16},{2,32},{3,48},{4,64},{5,80},{6,96},{7,112},{8,128},{9... | collective-permute-start | bytes 1179656 | tf_op jit(solution)/shard_map/ppermute | solution.py:57
  183.4 34.2 %copy-start.4 = (f32[512,1024]{1,0:T(8,128)S(1)}, f32[512,1024]{1,0:T(8,128)}, u32[]{:S(2)}) copy-start(f32[512,1024]{1,0:T(8,128)} %copy-done.3) | copy-start | bytes 6291460
  183.4 34.2 %copy-start.7 = (f32[512,1024]{1,0:T(8,128)S(1)}, f32[512,1024]{1,0:T(8,128)}, u32[]{:S(2)}) copy-start(f32[512,1024]{1,0:T(8,128)} %copy-done.6) | copy-start | bytes 6291460
  183.4 34.2 %copy-start.8 = (f32[512,1024]{1,0:T(8,128)S(1)}, f32[512,1024]{1,0:T(8,128)}, u32[]{:S(2)}) copy-start(f32[512,1024]{1,0:T(8,128)} %slice_bitcast_fusion.2) | copy-start | bytes 6291460
Sparse Core Ops, SparseCore 0:
  10.4 48.9 all-gather.1
  91.2 85.2 reduce-scatter.3
  224.6 96.3 all-reduce.2
where the time goes:
time: 338 us
  waiting for transfers between devices  246 us (73%)
  matrix products  53.1 us (16%)
  between operations  14 us (4%)
  local copies, waits for them, and re-layouts  12.4 us (4%)
  other arithmetic  7.1 us (2%)
  starting transfers between devices  5.08 us (2%)
    psum x1, waiting for transfers between devices, shards(): summed = lax.psum(jnp.concatenate([inner0, inner1, inner2], 1), 'prow')  92.2 us
    unnamed x4, waiting for transfers between devices  81.1 us
    all_gather x1, waiting for transfers between devices, shards(): f0, f1, f2 = lax.all_gather(factors, 'pcol', axis=1, tiled=True)  43.3 us
    dot_general x9, matrix products, mm(): jnp.dot(left, right, precision=precision, preferred_element_type=jnp.floa...  32.8 us
    ppermute x1, waiting for transfers between devices, shards(): xt = -lax.ppermute(mine, ('prow', 'pcol'), perm)  29.7 us
    dot_general x6, matrix products, tmm(): lax.dot_general(left, right, (((0,), (0,)), ((), ())), precision=precisio...  14.2 us
  transfers between devices with their start and end apart: 4, of which 4 were waited for; matrix products, arithmetic and copies ran while one was open for 6% of the time, Pallas kernels for 0%

commit v1 on v0

--- a/solution.py
+++ b/solution.py
@@ -42,7 +42,9 @@
     flags = lax.dynamic_slice_in_dim(pattern, row_index * blocks_here, blocks_here, 1)
     row_mask = jnp.repeat(flags.astype(jnp.float32), NB, axis=1)
     factors = jnp.swapaxes(panels, 1, 2) * row_mask[:, None, :]
-    f0, f1, f2 = lax.all_gather(factors, "pcol", axis=1, tiled=True)
+    f0, f1, f2 = jnp.concatenate(
+        lax.all_to_all(jnp.stack([factors] * lax.axis_size("pcol")), "pcol", 0, 0), axis=1
+    )
     c0, c1, c2 = (coupling[0], coupling[1], coupling[2])
     u01 = -c0
     u12 = -c2

time: 338 us -> 434 us (1.28)
  waiting for transfers between devices: 246 us -> 338 us
  starting transfers between devices: 5.08 us -> 13.8 us
  matrix products: 53.1 us -> 45.3 us
    all_to_all x0 -> x1, waiting for transfers between devices: none -> 134 us  [shards(): lax.all_to_all(jnp.stack([factors] * lax.axis_size('pcol')), 'pcol', 0, 0)]
    all_gather x1 -> x0, waiting for transfers between devices: 43.3 us -> none  [shards(): f0, f1, f2 = lax.all_gather(factors, 'pcol', axis=1, tiled=True)]
    all_to_all x0 -> x1, starting transfers between devices: none -> 8.75 us  [shards(): lax.all_to_all(jnp.stack([factors] * lax.axis_size('pcol')), 'pcol', 0, 0)]
    dot_general x9, matrix products: 32.8 us -> 27.3 us  [mm(): jnp.dot(left, right, precision=precision, preferred_element_type=jnp.floa...]
    unnamed x4 -> x3, waiting for transfers between devices: 81.1 us -> 81.5 us
  transfers between devices with their start and end apart: 4 -> 4, of which waited for: 4 -> 4; matrix products, arithmetic and copies ran while one was open for 6% -> 4% of each run, Pallas kernels for 0% -> 0%
where the time goes in v1:
time: 434 us; the launch traced here: 433 us
  waiting for transfers between devices  338 us (78%)
  matrix products  45.3 us (10%)
  local copies, waits for them, and re-layouts  15.9 us (4%)
  between operations  14.3 us (3%)
  starting transfers between devices  13.8 us (3%)
  other arithmetic  6.24 us (1%)
    all_to_all x1, waiting for transfers between devices, shards(): lax.all_to_all(jnp.stack([factors] * lax.axis_size('pcol')), 'pcol', 0, 0)  134 us
    psum x1, waiting for transfers between devices, shards(): summed = lax.psum(jnp.concatenate([inner0, inner1, inner2], 1), 'prow')  92.2 us
    unnamed x3, waiting for transfers between devices  81.5 us
    ppermute x1, waiting for transfers between devices, shards(): xt = -lax.ppermute(mine, ('prow', 'pcol'), perm)  29.7 us
    dot_general x9, matrix products, mm(): jnp.dot(left, right, precision=precision, preferred_element_type=jnp.floa...  27.3 us
    dot_general x6, matrix products, tmm(): lax.dot_general(left, right, (((0,), (0,)), ((), ())), precision=precisio...  12 us
    all_to_all x1, starting transfers between devices, shards(): lax.all_to_all(jnp.stack([factors] * lax.axis_size('pcol')), 'pcol', 0, 0)  8.75 us
  transfers between devices with their start and end apart: 4, of which 4 were waited for; matrix products, arithmetic and copies ran while one was open for 4% of the time, Pallas kernels for 0%

profile of v1, /device:TPU:2, one launch (start us, length us, event | category | flops | bytes accessed | tf_op | source)
XLA Modules:
  0.0 433.4 jit_solution(2624406265864404248)
XLA Ops:
  7.2 0.8 dynamic-slice_convert_fusion
  7.9 0.1 broadcast_bitcast_fusion
  8.0 1.0 multiply_bitcast_fusion
  9.0 3.4 stack.18
  12.5 8.7 %all-to-all-start = ((f32[16,3,32,1024]{3,2,1,0:T(8,128)}), f32[16,3,32,1024]{3,2,1,0:T(8,128)}, u32[]{:S(2)}, u32[]{:S(2)}) async-start(f32[16,3,32,1024]{3,2,1,0:T(8,128)} %stack.18), calls=%async_computation | async-start | bytes 12582912 | tf_op jit(solution)/shard_map/all_to_all | solution.py:46
  21.2 0.0 reduce-scatter.4.cloned.1.call-start
  21.3 0.3 copy.12
  21.6 4.4 %convolution_subtract_fusion = f32[512,512]{0,1:T(8,128)} fusion(f32[1,512,512]{1,2,0:T(8,128)S(1)} %copy.12, f32[3,512,512]{2,1,0:T(8,128)} %param.8), kind=kOutput, calls=%fused_computation.10 | convolution fusion | flops 1610874880 | bytes 4194304 | tf_op jit(solution)/shard_map/dot_general | solution.py:12
  26.0 134.5 %all-to-all-done = f32[16,3,32,1024]{3,2,1,0:T(8,128)} async-done(((f32[16,3,32,1024]{3,2,1,0:T(8,128)}), f32[16,3,32,1024]{3,2,1,0:T(8,128)}, u32[]{:S(2)}, u32[]{:S(2)}) %all-to-all-start) | async-done | bytes 6291488 | tf_op jit(solution)/shard_map/all_to_all | solution.py:46
  160.5 3.5 fusion.59
  164.0 0.0 copy-start
  164.1 1.9 fusion.62
  166.0 0.7 copy-done
  166.7 2.0 bitcast_add_fusion.2
  168.7 0.0 copy-start.7
  168.7 0.0 copy-start.9
  168.7 2.1 bitcast_add_fusion
  170.8 0.0 copy-done.3
  170.8 0.0 copy-done.7
  170.8 0.8 copy-done.9
  171.6 10.9 %fusion.1 = f32[1536,1024]{1,0:T(8,128)S(1)} fusion(f32[1024,1024]{1,0:T(8,128)S(1)} %copy-done.9, f32[512,1024]{1,0:T(8,128)S(1)} %bitcast_add_fusion, f32[512,1024]{1,0:T(8,128)S(1)} %bitcast_add_fusion.2, f32[512,1024]{1,0:T(8,128)S(1)} %bitcast.101), kind=kOutput, calls=%fused_computation.2 | convolution fusion | flops 9666822144 | bytes 16777216 | tf_op jit(solution)/shard_map/dot_general | solution.py:12
  182.6 3.2 copy.11
  185.8 0.0 reduce-scatter.4.cloned.1.call-update
  185.8 0.0 all-reduce.3.cloned.1.call-start
  185.9 1.2 bitcast_negate_fusion
  187.1 2.0 fusion.18
  189.1 1.0 fusion.63
  190.1 81.5 %reduce-scatter.4.cloned.1.call-done = f32[3,1,32,1024]{3,2,0,1:T(8,128)} async-done(((f32[3,16,32,1024]{3,2,0,1:T(8,128)}), f32[3,1,32,1024]{3,2,0,1:T(8,128)}) %reduce-scatter.4.cloned.1.call-update) | async-done | bytes 393232
  271.7 5.0 %collective-permute-start = (f32[3,32,1024]{2,1,0:T(8,128)}, f32[3,32,1024]{2,1,0:T(8,128)S(1)}, u32[]{:S(2)}, u32[]{:S(2)}) collective-permute-start(f32[3,32,1024]{2,1,0:T(8,128)} %bitcast.107), channel_id=1, source_target_pairs={{0,0},{1,16},{2,32},{3,48},{4,64},{5,80},{6,96},{7,112},{8,128},{9... | collective-permute-start | bytes 1179656 | tf_op jit(solution)/shard_map/ppermute | solution.py:59
  276.6 2.0 fusion.16
  278.6 3.7 fusion.60
  282.4 29.7 %collective-permute-done = f32[3,32,1024]{2,1,0:T(8,128)S(1)} collective-permute-done((f32[3,32,1024]{2,1,0:T(8,128)}, f32[3,32,1024]{2,1,0:T(8,128)S(1)}, u32[]{:S(2)}, u32[]{:S(2)}) %collective-permute-start) | collective-permute-done | bytes 393248 | tf_op jit(solution)/shard_map/ppermute | solution.py:59
  312.1 0.8 fusion.61
  312.9 3.0 fusion
  315.8 2.0 fusion.2
  317.9 1.1 fusion.38
  318.9 0.8 pad_maximum_fusion.3
  319.7 0.0 all-reduce.3.cloned.1.call-update
  319.7 2.1 fusion.14
  321.8 2.3 convolution_add_fusion.1
  324.1 92.2 %all-reduce.3.cloned.1.call-done = f32[32,3072]{1,0:T(8,128)} async-done(((f32[32,3072]{1,0:T(8,128)}), f32[32,3072]{1,0:T(8,128)}) %all-reduce.3.cloned.1.call-update) | async-done | bytes 393232 | tf_op jit(solution)/shard_map/psum | solution.py:63
  416.2 2.3 fusion.12
  418.5 1.6 fusion.13
  420.1 0.9 fusion.39
  421.0 1.6 fusion.9
  422.6 1.6 fusion.11
  424.2 1.6 fusion.7
  425.8 0.8 pad_maximum_fusion.4
  (16 shorter events, 0.0 us)
Async XLA Ops:
  12.5 8.8 %slice-start = ((f32[3,512,512]{2,1,0:T(8,128)}), f32[1,512,512]{2,1,0:T(8,128)S(1)}, s32[]{:S(2)}) async-start(f32[3,512,512]{2,1,0:T(8,128)} %param.8), calls=%async_computation.4 | async-start | bytes 2097152 | tf_op jit(solution)/shard_map/slice | solution.py:48
  12.5 148.0 %all-to-all-start = ((f32[16,3,32,1024]{3,2,1,0:T(8,128)}), f32[16,3,32,1024]{3,2,1,0:T(8,128)}, u32[]{:S(2)}, u32[]{:S(2)}) async-start(f32[16,3,32,1024]{3,2,1,0:T(8,128)} %stack.18), calls=%async_computation | async-start | bytes 12582912 | tf_op jit(solution)/shard_map/all_to_all | solution.py:46
  21.2 250.4 %reduce-scatter.4.cloned.1.call-start = ((), (), s32[]{:S(2)}) async-start(), calls=%async_computation.3 | async-start | bytes 6684672
  160.5 3.6 copy-start.1
  164.0 6.7 %copy-start.3 = (f32[1,16,32,1024]{3,2,0,1:T(8,128)}, f32[1,16,32,1024]{3,2,0,1:T(8,128)S(1)}, u32[]{:S(2)}) copy-start(f32[1,16,32,1024]{3,2,0,1:T(8,128)S(1)} %get-tuple-element.5) | copy-start | bytes 6291460
  164.0 2.6 copy-start
  168.7 2.1 copy-start.7
  168.7 2.9 copy-start.9
  171.6 10.9 %copy-start.5 = (f32[512,1024]{1,0:T(8,128)}, f32[512,1024]{1,0:T(8,128)S(1)}, u32[]{:S(2)}) copy-start(f32[512,1024]{1,0:T(8,128)S(1)} %bitcast_add_fusion) | copy-start | bytes 6291460
  185.8 230.4 %all-reduce.3.cloned.1.call-start = ((), (), s32[]{:S(2)}) async-start(), calls=%async_computation.2 | async-start | bytes 786432 | tf_op jit(solution)/shard_map/psum | solution.py:63
  185.9 3.2 copy-start.2
  271.7 40.4 %collective-permute-start = (f32[3,32,1024]{2,1,0:T(8,128)}, f32[3,32,1024]{2,1,0:T(8,128)S(1)}, u32[]{:S(2)}, u32[]{:S(2)}) collective-permute-start(f32[3,32,1024]{2,1,0:T(8,128)} %bitcast.107), channel_id=1, source_target_pairs={{0,0},{1,16},{2,32},{3,48},{4,64},{5,80},{6,96},{7,112},{8,128},{9... | collective-permute-start | bytes 1179656 | tf_op jit(solution)/shard_map/ppermute | solution.py:59
  278.6 34.3 %copy-start.4 = (f32[1,16,32,1024]{3,2,0,1:T(8,128)S(1)}, f32[1,16,32,1024]{3,2,0,1:T(8,128)}, u32[]{:S(2)}) copy-start(f32[1,16,32,1024]{3,2,0,1:T(8,128)} %copy-done.3) | copy-start | bytes 6291460
  278.6 34.3 %copy-start.6 = (f32[512,1024]{1,0:T(8,128)S(1)}, f32[512,1024]{1,0:T(8,128)}, u32[]{:S(2)}) copy-start(f32[512,1024]{1,0:T(8,128)} %copy-done.5) | copy-start | bytes 6291460
  278.6 34.2 %copy-start.8 = (f32[512,1024]{1,0:T(8,128)S(1)}, f32[512,1024]{1,0:T(8,128)}, u32[]{:S(2)}) copy-start(f32[512,1024]{1,0:T(8,128)} %copy-done.7) | copy-start | bytes 6291460
Sparse Core Ops, SparseCore 0:
  185.9 85.6 reduce-scatter.3
  319.9 96.3 all-reduce.2
